TPU v7x, 256 devices: a whole 4x4x8 slice. The times are simulated.
256 devices in a mesh: row: 16 (over y, x), col: 16 (over z, core).
Axes of the slice: x: 4, y: 4, z: 8, core: 2. Of those that a mesh axis runs over, the one named last changes fastest.
Arguments:
- trailing_slab: bfloat16 [98304, 8192], P('row', 'col'), may hold values from -6 to 6
- panel_cols: bfloat16 [98304, 512], P('row', 'col'), may hold values from -0.25 to 0.25
- head_slab: bfloat16 [512, 8192], P('row', 'col'), may hold values from -6 to 6
- coupling: bfloat16 [2, 256, 256], replicated, may hold values from -0.25 to 0.25
- lower_inverses: bfloat16 [2, 256, 256], replicated, may hold values from -1.5 to 1.5, as said below
- upper_inverses: bfloat16 [2, 256, 256], replicated, may hold values from -1.5 to 1.5, as said below
Outputs:
- trailing: bfloat16 [98304, 8192], P('row', 'col')
Inputs may be any that keep to these rules, and one draw needn't show every extreme that they name: `lower_inverses`: each of the two [256, 256] blocks is lower triangular with unit diagonal. `upper_inverses`: each of the two [256, 256] blocks is upper triangular with diagonal between 0.5 and 1.5.
All inputs are finite; a program needn't handle non-finite values.
Results may differ from a plain program's by a relative error of at most 0.0067.
Values may be sent and summed in bfloat16 or wider, within the bound.
A program may use at most 128 MiB of HBM per device.

v0:
```python
import jax
import jax.numpy as jnp
from jax import lax
from jax.sharding import PartitionSpec as P


def product(left, right):
    return jnp.dot(left, right, preferred_element_type=jnp.float32)


def factor_panel(panel_block, upper_mid, upper_inverses):
    width = upper_mid.shape[0]
    lower_first = product(panel_block[:, :width], upper_inverses[0]).astype(jnp.bfloat16)
    panel_second = (
        panel_block[:, width:].astype(jnp.float32) - product(lower_first, upper_mid)
    ).astype(jnp.bfloat16)
    lower_second = product(panel_second, upper_inverses[1]).astype(jnp.bfloat16)
    return jnp.concatenate([lower_first, lower_second], axis=1)


def apply_update(slab_part, lower_block, upper_first, upper_second):
    width = upper_first.shape[0]
    result = slab_part.astype(jnp.float32) - product(lower_block[:, :width], upper_first)
    result = result - product(lower_block[:, width:], upper_second)
    return result.astype(jnp.bfloat16)


def on_device(trailing_slab, panel_cols, head_slab, coupling, lower_inverses, upper_inverses):
    width = coupling.shape[1]
    head_full = lax.all_gather(head_slab, "row", axis=0, tiled=True)
    upper_mid = product(lower_inverses[0], coupling[0]).astype(jnp.bfloat16)
    upper_first = product(lower_inverses[0], head_full[:width]).astype(jnp.bfloat16)
    lower_head = product(coupling[1], upper_inverses[0]).astype(jnp.bfloat16)
    head_second = (head_full[width:].astype(jnp.float32) - product(lower_head, upper_first)).astype(
        jnp.bfloat16
    )
    upper_second = product(lower_inverses[1], head_second).astype(jnp.bfloat16)
    panel_full = lax.all_gather(panel_cols, "col", axis=1, tiled=True)
    lower_block = factor_panel(panel_full, upper_mid, upper_inverses)
    return apply_update(trailing_slab, lower_block, upper_first, upper_second)


def solution(mesh):
    in_specs = (P("row", "col"), P("row", "col"), P("row", "col"), P(), P(), P())
    out_specs = P("row", "col")
    return jax.shard_map(
        on_device, mesh=mesh, in_specs=in_specs, out_specs=out_specs, check_vma=False
    )
```

profile of v0, /device:TPU:1, one launch (start us, length us, event | category | flops | bytes accessed | tf_op | source)
XLA Modules:
  0.0 92.3 jit_solution(4468652648620062234)
XLA Ops:
  6.5 0.0 all-gather.2.cloned.1.call-start
  6.5 0.7 all-gather.2.cloned.1.call-update
  7.3 20.1 %all_gather.7 = bf16[512,512]{1,0:T(8,128)(2,1)S(1)} all-gather(bf16[32,512]{1,0:T(8,128)(2,1)} %param.8), channel_id=1, replica_groups=mesh['row'=16,'col'=16] {'row'}, dimensions={0}, use_global_device_ids=true | all-gather | bytes 557056 | tf_op jit(solution)/shard_map/all_gather | solution.py:30
  27.3 1.2 %convolution_convert_fusion.4 = bf16[256,256]{1,0:T(8,128)(2,1)S(1)} fusion(bf16[2,256,256]{2,1,0:T(8,128)(2,1)} %param.9, bf16[2,256,256]{2,1,0:T(8,128)(2,1)} %param.11), kind=kOutput, calls=%fused_computation.10 | convolution fusion | flops 33619968 | bytes 393216 | tf_op jit(solution)/shard_map/dot_general | solution.py:8
  28.5 1.2 %convolution_convert_fusion.5 = bf16[256,256]{1,0:T(8,128)(2,1)S(1)} fusion(bf16[2,256,256]{2,1,0:T(8,128)(2,1)} %param.9, bf16[2,256,256]{2,1,0:T(8,128)(2,1)} %param.10), kind=kOutput, calls=%fused_computation.11 | convolution fusion | flops 33619968 | bytes 393216 | tf_op jit(solution)/shard_map/dot_general | solution.py:8
  29.6 1.1 %convolution_convert_fusion.3 = bf16[256,512]{1,0:T(8,128)(2,1)S(1)} fusion(bf16[512,512]{1,0:T(8,128)(2,1)S(1)} %all_gather.7, bf16[2,256,256]{2,1,0:T(8,128)(2,1)} %param.10), kind=kOutput, calls=%fused_computation.8 | convolution fusion | flops 67239936 | bytes 655360 | tf_op jit(solution)/shard_map/dot_general | solution.py:8
  30.8 2.1 %convolution_convert_fusion.2 = bf16[512,256]{1,0:T(8,128)(2,1)} fusion(bf16[256,256]{1,0:T(8,128)(2,1)S(1)} %convolution_convert_fusion.4, bf16[256,512]{1,0:T(8,128)(2,1)S(1)} %convolution_convert_fusion.3, bf16[512,512]{1,0:T(8,128)(2,1)S(1)} %all_gather.7, bf16[2,256,256]{2,1,0:T(8,128)(2,1)} %param.10), kind=kOutput, calls=%fused_computation.7 | convolution fusion | flops 134742016 | bytes 1048576 | tf_op jit(solution)/shard_map/dot_general | solution.py:8
  32.9 26.6 %all-gather.2.cloned.1.call-done = bf16[6144,512]{0,1:T(8,128)(2,1)} async-done(((bf16[6144,32]{0,1:T(8,128)(2,1)}), bf16[6144,512]{0,1:T(8,128)(2,1)}) %all-gather.2.cloned.1.call-update) | async-done | bytes 6291472 | tf_op jit(solution)/shard_map/all_gather | solution.py:38
  59.5 2.9 %convolution_convert_fusion.1 = bf16[6144,256]{1,0:T(8,128)(2,1)S(1)} fusion(bf16[6144,512]{0,1:T(8,128)(2,1)} %all-gather.2.cloned.1.call-done, bf16[2,256,256]{2,1,0:T(8,128)(2,1)} %param.11), kind=kOutput, calls=%fused_computation.4 | convolution fusion | flops 806879232 | bytes 6422528 | tf_op jit(solution)/shard_map/dot_general | solution.py:8
  62.4 6.3 %fusion.22 = f32[6144,512]{1,0:T(8,128)} fusion(bf16[6144,256]{1,0:T(8,128)(2,1)S(1)} %convolution_convert_fusion.1, bf16[256,512]{1,0:T(8,128)(2,1)S(1)} %convolution_convert_fusion.3), kind=kOutput, calls=%fused_computation.31 | convolution fusion | flops 1610612736 | bytes 15990784 | tf_op jit(solution)/shard_map/dot_general | solution.py:8
  68.7 0.0 copy-start
  68.8 5.6 %convolution_convert_fusion = bf16[6144,256]{1,0:T(8,128)(2,1)} fusion(bf16[6144,256]{1,0:T(8,128)(2,1)S(1)} %convolution_convert_fusion.1, bf16[256,256]{1,0:T(8,128)(2,1)S(1)} %convolution_convert_fusion.5, bf16[6144,512]{0,1:T(8,128)(2,1)} %all-gather.2.cloned.1.call-done, bf16[2,256,256]{2,1,0:T(8,128)(2,1)} %param.11), kind=kOutput, calls=%fused_computation.3 | convolution fusion | flops 1616904192 | bytes 9699328 | tf_op jit(solution)/shard_map/dot_general | solution.py:8
  74.3 0.0 copy-done
  74.3 11.1 %subtract_convert_fusion = bf16[6144,512]{1,0:T(8,128)(2,1)} fusion(f32[6144,512]{1,0:T(8,128)} %fusion.22, bf16[6144,512]{1,0:T(8,128)(2,1)} %param.6, bf16[6144,256]{1,0:T(8,128)(2,1)} %convolution_convert_fusion, bf16[512,256]{1,0:T(8,128)(2,1)S(1)} %copy-done), kind=kOutput, calls=%fused_computation | convolution fusion | flops 1623195648 | bytes 28573696 | tf_op jit(solution)/shard_map/dot_general | solution.py:8
Async XLA Ops:
  6.5 52.9 %all-gather.2.cloned.1.call-start = ((), (), s32[]{:S(2)}) async-start(), calls=%async_computation | async-start | bytes 6684672 | tf_op jit(solution)/shard_map/all_gather | solution.py:38
  68.7 5.6 %copy-start = (bf16[512,256]{1,0:T(8,128)(2,1)S(1)}, bf16[512,256]{1,0:T(8,128)(2,1)}, u32[]{:S(2)}) copy-start(bf16[512,256]{1,0:T(8,128)(2,1)} %convolution_convert_fusion.2) | copy-start | bytes 786436
Sparse Core Ops, SparseCore 0:
  9.2 50.2 all-gather.1
where the time goes:
time: 92.5 us; the launch traced here: 92.3 us
  matrix products  31.5 us (34%)
  waiting for transfers between devices  27.3 us (30%)
  blocking collectives  20.1 us (22%)
  between operations  13.4 us (14%)
    dot_general x8, matrix products, product(): return jnp.dot(left, right, preferred_element_type=jnp.float32)  31.5 us
    all_gather x1, waiting for transfers between devices, on_device(): panel_full = lax.all_gather(panel_cols, 'col', axis=1, tiled=True)  26.6 us
    all_gather x1, blocking collectives, on_device(): head_full = lax.all_gather(head_slab, 'row', axis=0, tiled=True)  20.1 us
  transfers between devices with their start and end apart: 1, of which 1 were waited for; matrix products, arithmetic and copies ran while one was open for 6% of the time, Pallas kernels for 0%

commit v1 on v0

v1 whole, which is shorter than its diff:
```python
import functools

import jax
import jax.numpy as jnp
from jax import lax
from jax.experimental import pallas as pl
from jax.experimental.pallas import tpu as pltpu
from jax.sharding import PartitionSpec as P

MESH = pl.DeviceIdType.MESH
BF16 = jnp.bfloat16
F32 = jnp.float32
BATCH = 8
CHUNKS = 2 * BATCH
DEPTH = 8


def product(left, right):
    return jnp.dot(left, right, preferred_element_type=F32)


def update_kernel(
    slab_hbm, panel_hbm, head_hbm, coupling_hbm, lower_hbm, upper_hbm,
    out,
    gathered, head_full, coupling, lower_inv, upper_inv, mid, factors,
    local_sem, ring_send, pair_send, head_send, ring_recv, pair_recv, head_recv,
):
    chunks, width2, rows = gathered.shape
    width = width2 // 2
    share = panel_hbm.shape[0]
    head_share = head_hbm.shape[0]
    row = lax.axis_index("row")
    col = lax.axis_index("col")
    n_row = lax.axis_size("row")
    depth = lax.axis_size("col") // 2
    z, core = col // 2, col % 2
    ahead = ((z + 1) % depth) * 2 + core
    behind = ((z + depth - 1) % depth) * 2 + core
    other = z * 2 + (1 - core)

    barrier = pltpu.get_barrier_semaphore()
    for peer in (ahead, behind, other):
        pl.semaphore_signal(barrier, inc=1, device_id=(row, peer), device_id_type=MESH)
    for step in range(1, n_row):
        pl.semaphore_signal(
            barrier, inc=1, device_id=((row + step) % n_row, col), device_id_type=MESH
        )

    def block_rows(hops):
        source = ((z + depth - hops) % depth) * 2 + core
        return pl.ds(pl.multiple_of(source * share, share), share)

    own_rows = block_rows(0)
    head_rows = pl.ds(pl.multiple_of(row * head_share, head_share), head_share)

    for chunk in range(chunks):
        pltpu.make_async_copy(
            panel_hbm.at[:, pl.ds(chunk * rows, rows)],
            gathered.at[chunk, own_rows],
            local_sem.at[0],
        ).start()
    head_copy = pltpu.make_async_copy(head_hbm, head_full.at[head_rows], local_sem.at[1])
    head_copy.start()
    small_copies = [
        pltpu.make_async_copy(source, target, local_sem.at[at])
        for source, target, at in (
            (coupling_hbm, coupling, 2), (lower_hbm, lower_inv, 3), (upper_hbm, upper_inv, 4),
            (slab_hbm, out, 5),
        )
    ]
    for copy in small_copies:
        copy.start()
    pltpu.make_async_copy(
        gathered.at[:, own_rows], gathered.at[:, own_rows], local_sem.at[0]
    ).wait()
    head_copy.wait()
    pl.semaphore_wait(barrier, 3 + n_row - 1)

    def ring_copy(direction, hop, chunk):
        hops = hop - 1 if direction == 0 else depth - (hop - 1)
        where = block_rows(hops)
        return pltpu.make_async_remote_copy(
            src_ref=gathered.at[chunk, where],
            dst_ref=gathered.at[chunk, where],
            send_sem=ring_send,
            recv_sem=ring_recv.at[direction, hop - 1, chunk],
            device_id=(row, ahead if direction == 0 else behind),
            device_id_type=MESH,
        )

    def ring_arrived(direction, hop, chunk):
        hops = hop if direction == 0 else depth - hop
        where = block_rows(hops)
        pltpu.make_async_remote_copy(
            src_ref=gathered.at[chunk, where],
            dst_ref=gathered.at[chunk, where],
            send_sem=ring_send,
            recv_sem=ring_recv.at[direction, hop - 1, chunk],
            device_id=(row, ahead if direction == 0 else behind),
            device_id_type=MESH,
        ).wait_recv()

    def pair_copy(direction, hop, chunk):
        hops = hop if direction == 0 else depth - hop
        where = block_rows(hops)
        return pltpu.make_async_remote_copy(
            src_ref=gathered.at[chunk, where],
            dst_ref=gathered.at[chunk, where],
            send_sem=pair_send,
            recv_sem=pair_recv.at[chunk],
            device_id=(row, other),
            device_id_type=MESH,
        )

    def send_own(chunk):
        ring_copy(0, 1, chunk).start()
        ring_copy(1, 1, chunk).start()
        pair_copy(0, 0, chunk).start()

    def forward(direction, hop, chunk):
        ring_arrived(direction, hop, chunk)
        ring_copy(direction, hop + 1, chunk).start()
        pair_copy(direction, hop, chunk).start()

    def keep(direction, hop, chunk):
        ring_arrived(direction, hop, chunk)
        pair_copy(direction, hop, chunk).start()

    half = BATCH // 2

    def compute(chunk):
        every = pl.ds(0, width2)
        other_half = gathered.at[chunk, pl.ds(0, width)]
        pltpu.make_async_copy(other_half, other_half, pair_recv.at[chunk]).wait()
        panel = gathered[chunk].T
        lower_first = product(panel[:, :width], upper_inv[0]).astype(BF16)
        second = (panel[:, width:].astype(F32) - product(lower_first, mid[...])).astype(BF16)
        lower_second = product(second, upper_inv[1]).astype(BF16)
        lower_block = jnp.concatenate([lower_first, lower_second], axis=1)
        where = pl.ds(pl.multiple_of(chunk * rows, rows), rows)
        out[where, :] = (
            out[where, :].astype(F32) - product(lower_block, factors[...])
        ).astype(BF16)

    def loop(count, body):
        lax.fori_loop(0, count, lambda i, carry: (body(i), carry)[1], 0)

    loop(BATCH, send_own)
    for step in range(1, n_row):
        pltpu.make_async_remote_copy(
            src_ref=head_full.at[head_rows],
            dst_ref=head_full.at[head_rows],
            send_sem=head_send,
            recv_sem=head_recv,
            device_id=((row + step) % n_row, col),
            device_id_type=MESH,
        ).start()
    for copy in small_copies:
        copy.wait()
    mid[...] = product(lower_inv[0], coupling[0]).astype(BF16)
    lower_head = product(coupling[1], upper_inv[0]).astype(BF16)

    def second_hop(chunk):
        forward(0, 1, chunk)
        forward(1, 1, chunk)

    def third_hop(base):
        def body(i):
            forward(0, 2, base + (2 * i) % BATCH + (2 * i) // BATCH)
            forward(1, 2, base + (2 * i + 1) % BATCH - (2 * i) // BATCH)
        return body

    loop(BATCH, second_hop)

    others = head_full.at[pl.ds(0, head_share * (n_row - 1))]
    pltpu.make_async_copy(others, others, head_recv).wait()
    upper_first = product(lower_inv[0], head_full[:width]).astype(BF16)
    head_second = (
        head_full[width:].astype(F32) - product(lower_head, upper_first)
    ).astype(BF16)
    factors[:width] = upper_first
    factors[width:] = product(lower_inv[1], head_second).astype(BF16)

    loop(BATCH, third_hop(0))

    def last_hop(base, next_base):
        def body(i):
            even, odd = base + 2 * i, base + 2 * i + 1
            if next_base is not None:
                send_own(next_base + 2 * i)
            forward(0, 3, even)
            forward(1, 3, odd)
            if next_base is not None:
                send_own(next_base + 2 * i + 1)
        return body

    def last_keep(base):
        def body(i):
            even, odd = base + 2 * i, base + 2 * i + 1
            keep(1, 3, even)
            keep(0, 3, odd)
        return body

    loop(half, last_hop(0, BATCH))
    loop(half, last_keep(0))

    def finish(base):
        def body(i):
            keep(0, 4, base + 2 * i)
            keep(1, 4, base + 2 * i + 1)
        return body

    def second_hop_late(i):
        second_hop(BATCH + i)

    loop(half, second_hop_late)
    loop(half, finish(0))

    def second_hop_compute(i):
        second_hop(BATCH + half + i)
        compute(i)

    loop(half, second_hop_compute)

    third = third_hop(BATCH)
    loop(half, third)

    def third_hop_compute(i):
        third(half + i)
        compute(half + i)

    loop(half, third_hop_compute)
    loop(half, last_hop(BATCH, None))
    loop(half, last_keep(BATCH))
    finish(BATCH)(0)

    done = finish(BATCH)

    def done_compute(i):
        done(i + 1)
        compute(BATCH + 2 * i)
        compute(BATCH + 2 * i + 1)

    loop(half - 1, done_compute)
    compute(CHUNKS - 2)
    compute(CHUNKS - 1)

    sent = gathered.at[:, pl.ds(0, share * (depth - 1))]
    pltpu.make_async_copy(sent, sent, ring_send).wait()
    shared = gathered.at[:, pl.ds(0, share * depth)]
    pltpu.make_async_copy(shared, shared, pair_send).wait()
    pltpu.make_async_copy(others, others, head_send).wait()


def write_kernel(result, out, sem):
    parts = 8
    rows = result.shape[0] // parts
    copies = [
        pltpu.make_async_copy(
            result.at[pl.ds(at * rows, rows)], out.at[pl.ds(at * rows, rows)], sem.at[at]
        )
        for at in range(parts)
    ]
    for copy in copies:
        copy.start()
    for copy in copies:
        copy.wait()


def on_device(trailing_slab, panel_cols, head_slab, coupling, lower_inverses, upper_inverses):
    height, columns = trailing_slab.shape
    width = coupling.shape[1]
    rows = height // CHUNKS
    dma = pltpu.SemaphoreType.DMA
    anywhere = pl.BlockSpec(memory_space=pltpu.HBM)
    result = pl.pallas_call(
        update_kernel,
        out_shape=jax.ShapeDtypeStruct((height, columns), BF16),
        in_specs=[anywhere] * 6,
        out_specs=pl.BlockSpec(memory_space=pltpu.VMEM),
        scratch_shapes=[
            pltpu.VMEM((CHUNKS, 2 * width, rows), BF16),
            pltpu.VMEM((2 * width, columns), BF16),
            pltpu.VMEM(coupling.shape, BF16),
            pltpu.VMEM(lower_inverses.shape, BF16),
            pltpu.VMEM(upper_inverses.shape, BF16),
            pltpu.VMEM((width, width), BF16),
            pltpu.VMEM((2 * width, columns), BF16),
            dma((6,)),
            dma(()),
            dma(()),
            dma(()),
            dma((2, 4, CHUNKS)),
            dma((CHUNKS,)),
            dma(()),
        ],
        compiler_params=pltpu.CompilerParams(
            collective_id=0, has_side_effects=True, vmem_limit_bytes=40 << 20
        ),
        name="gather_and_update",
    )(*[
        pltpu.with_memory_space_constraint(value, pltpu.HBM)
        for value in (
            trailing_slab, panel_cols.T, head_slab, coupling, lower_inverses, upper_inverses
        )
    ])
    return pl.pallas_call(
        write_kernel,
        out_shape=jax.ShapeDtypeStruct((height, columns), BF16),
        in_specs=[pl.BlockSpec(memory_space=pltpu.VMEM)],
        out_specs=anywhere,
        scratch_shapes=[dma((8,))],
        compiler_params=pltpu.CompilerParams(vmem_limit_bytes=16 << 20),
        name="write_result",
    )(result)


def solution(mesh):
    in_specs = (P("row", "col"), P("row", "col"), P("row", "col"), P(), P(), P())
    out_specs = P("row", "col")
    return jax.shard_map(
        on_device, mesh=mesh, in_specs=in_specs, out_specs=out_specs, check_vma=False
    )
```

time: 92.5 us -> 56.3 us (0.61)
  Pallas kernels: 0 us -> 56.2 us
  matrix products: 31.5 us -> 0 us
  waiting for transfers between devices: 27.3 us -> 0 us
  blocking collectives: 20.1 us -> 0 us
  between operations: 13.4 us -> 0.01 us
    pallas_call x0 -> x2, Pallas kernels: none -> 56.2 us  [the longest x1 53.5 us: on_device(): pl.pallas_call(update_kernel, out_shape=jax.ShapeDtypeStruct((height, col...]
    dot_general x8 -> x0, matrix products: 31.5 us -> none  [product(): return jnp.dot(left, right, preferred_element_type=jnp.float32)]
    all_gather x1 -> x0, waiting for transfers between devices: 26.6 us -> none  [on_device(): panel_full = lax.all_gather(panel_cols, 'col', axis=1, tiled=True)]
    all_gather x1 -> x0, blocking collectives: 20.1 us -> none  [on_device(): head_full = lax.all_gather(head_slab, 'row', axis=0, tiled=True)]
  transfers between devices with their start and end apart: 1 -> 0, of which waited for: 1 -> 0; matrix products, arithmetic and copies ran while one was open for 6% -> 0% of each run, Pallas kernels for 0% -> 0%
where the time goes in v1:
time: 56.3 us; the launch traced here: 56.2 us
  Pallas kernels  56.2 us (100%)
    pallas_call x1, Pallas kernels, on_device(): pl.pallas_call(update_kernel, out_shape=jax.ShapeDtypeStruct((height, col...  53.5 us
    pallas_call x1, Pallas kernels, on_device(): pl.pallas_call(write_kernel, out_shape=jax.ShapeDtypeStruct((height, colu...  2.74 us

profile of v1, /device:TPU:1, one launch (start us, length us, event | category | flops | bytes accessed | tf_op | source)
XLA Modules:
  0.0 56.2 jit_solution(7867515575170133723)
XLA Ops:
  0.0 53.5 %gather_and_update.1.result = bf16[6144,512]{1,0:T(8,128)(2,1)S(1)} custom-call(bf16[6144,512]{1,0:T(8,128)(2,1)} %slab_hbm.1, bf16[32,6144]{1,0:T(8,128)(2,1)} %bitcast.1, bf16[32,512]{1,0:T(8,128)(2,1)} %head_hbm.1, bf16[2,256,256]{2,1,0:T(8,128)(2,1)} %coupling_hbm.1, bf16[2,256,256]{2,1,0:T(8,128)(2,1)} %lower_hbm.1, bf16[2,256,256]{2,1,0:T(8,128)(2,1)} %upper_hbm.1), custom_call_target="tpu_custom_call" | custom-call | tf_op jit(solution)/shard_map/gather_and_update/pallas_call | solution.py:276
  53.5 2.7 %write_result.1 = bf16[6144,512]{1,0:T(8,128)(2,1)} custom-call(bf16[6144,512]{1,0:T(8,128)(2,1)S(1)} %gather_and_update.1.result), custom_call_target="tpu_custom_call" | custom-call | tf_op jit(solution)/shard_map/write_result/pallas_call | solution.py:307

commit v2 on v1

--- a/solution.py
+++ b/solution.py
@@ -10,19 +10,29 @@
 MESH = pl.DeviceIdType.MESH
 BF16 = jnp.bfloat16
 F32 = jnp.float32
-BATCH = 8
-CHUNKS = 2 * BATCH
-DEPTH = 8
+GROUP = 4
+GROUPS = 3
+CHUNKS = GROUP * GROUPS
 
 
 def product(left, right):
     return jnp.dot(left, right, preferred_element_type=F32)
 
 
+def updated_rows(gathered, chunk, slab_part, upper_inv, mid, factors):
+    width = mid.shape[0]
+    panel = jnp.concatenate([gathered[chunk].T, gathered[chunk + 1].T], axis=0)
+    lower_first = product(panel[:, :width], upper_inv[0]).astype(BF16)
+    second = (panel[:, width:].astype(F32) - product(lower_first, mid[...])).astype(BF16)
+    lower_second = product(second, upper_inv[1]).astype(BF16)
+    lower_block = jnp.concatenate([lower_first, lower_second], axis=1)
+    return (slab_part.astype(F32) - product(lower_block, factors[...])).astype(BF16)
+
+
 def update_kernel(
     slab_hbm, panel_hbm, head_hbm, coupling_hbm, lower_hbm, upper_hbm,
-    out,
-    gathered, head_full, coupling, lower_inv, upper_inv, mid, factors,
+    out, gathered, upper_inv, mid, factors,
+    head_full, coupling, lower_inv,
     local_sem, ring_send, pair_send, head_send, ring_recv, pair_recv, head_recv,
 ):
     chunks, width2, rows = gathered.shape
@@ -126,26 +136,55 @@
         ring_arrived(direction, hop, chunk)
         pair_copy(direction, hop, chunk).start()
 
-    half = BATCH // 2
-
-    def compute(chunk):
-        every = pl.ds(0, width2)
+    def pair_arrived(chunk):
         other_half = gathered.at[chunk, pl.ds(0, width)]
         pltpu.make_async_copy(other_half, other_half, pair_recv.at[chunk]).wait()
-        panel = gathered[chunk].T
-        lower_first = product(panel[:, :width], upper_inv[0]).astype(BF16)
-        second = (panel[:, width:].astype(F32) - product(lower_first, mid[...])).astype(BF16)
-        lower_second = product(second, upper_inv[1]).astype(BF16)
-        lower_block = jnp.concatenate([lower_first, lower_second], axis=1)
-        where = pl.ds(pl.multiple_of(chunk * rows, rows), rows)
-        out[where, :] = (
-            out[where, :].astype(F32) - product(lower_block, factors[...])
-        ).astype(BF16)
+
+    def update(group, i):
+        chunk = group * GROUP + 2 * i
+        pair_arrived(chunk)
+        pair_arrived(chunk + 1)
+        where = pl.ds(pl.multiple_of(chunk * rows, rows), 2 * rows)
+        out[where, :] = updated_rows(gathered, chunk, out[where, :], upper_inv, mid, factors)
 
     def loop(count, body):
         lax.fori_loop(0, count, lambda i, carry: (body(i), carry)[1], 0)
 
-    loop(BATCH, send_own)
+    def second(group, i):
+        forward(0, 1, group * GROUP + i)
+        forward(1, 1, group * GROUP + i)
+
+    def third(group, i):
+        base = group * GROUP
+        turn = (2 * i) // GROUP
+        forward(0, 2, base + (2 * i) % GROUP + turn)
+        forward(1, 2, base + (2 * i + 1) % GROUP - turn)
+
+    def fourth(group, i):
+        forward(0, 3, group * GROUP + 2 * i)
+        forward(1, 3, group * GROUP + 2 * i + 1)
+
+    def keep_third(group, i):
+        keep(1, 3, group * GROUP + 2 * i)
+        keep(0, 3, group * GROUP + 2 * i + 1)
+
+    def keep_fourth(group, i):
+        keep(0, 4, group * GROUP + 2 * i)
+        keep(1, 4, group * GROUP + 2 * i + 1)
+
+    def finish(group, i):
+        keep_third(group, i)
+        keep_fourth(group, i)
+
+    def run(count, *bodies):
+        def body(i):
+            for step, group in bodies:
+                step(group, i)
+        loop(count, body)
+
+    half = GROUP // 2
+
+    loop(2 * GROUP, send_own)
     for step in range(1, n_row):
         pltpu.make_async_remote_copy(
             src_ref=head_full.at[head_rows],
@@ -160,17 +199,8 @@
     mid[...] = product(lower_inv[0], coupling[0]).astype(BF16)
     lower_head = product(coupling[1], upper_inv[0]).astype(BF16)
 
-    def second_hop(chunk):
-        forward(0, 1, chunk)
-        forward(1, 1, chunk)
-
-    def third_hop(base):
-        def body(i):
-            forward(0, 2, base + (2 * i) % BATCH + (2 * i) // BATCH)
-            forward(1, 2, base + (2 * i + 1) % BATCH - (2 * i) // BATCH)
-        return body
-
-    loop(BATCH, second_hop)
+    run(GROUP, (second, 0), (lambda group, i: send_own(group * GROUP + i), 2))
+    run(GROUP, (third, 0), (second, 1))
 
     others = head_full.at[pl.ds(0, head_share * (n_row - 1))]
     pltpu.make_async_copy(others, others, head_recv).wait()
@@ -181,69 +211,21 @@
     factors[:width] = upper_first
     factors[width:] = product(lower_inv[1], head_second).astype(BF16)
 
-    loop(BATCH, third_hop(0))
-
-    def last_hop(base, next_base):
-        def body(i):
-            even, odd = base + 2 * i, base + 2 * i + 1
-            if next_base is not None:
-                send_own(next_base + 2 * i)
-            forward(0, 3, even)
-            forward(1, 3, odd)
-            if next_base is not None:
-                send_own(next_base + 2 * i + 1)
-        return body
-
-    def last_keep(base):
-        def body(i):
-            even, odd = base + 2 * i, base + 2 * i + 1
-            keep(1, 3, even)
-            keep(0, 3, odd)
-        return body
-
-    loop(half, last_hop(0, BATCH))
-    loop(half, last_keep(0))
-
-    def finish(base):
-        def body(i):
-            keep(0, 4, base + 2 * i)
-            keep(1, 4, base + 2 * i + 1)
-        return body
-
-    def second_hop_late(i):
-        second_hop(BATCH + i)
-
-    loop(half, second_hop_late)
-    loop(half, finish(0))
-
-    def second_hop_compute(i):
-        second_hop(BATCH + half + i)
-        compute(i)
-
-    loop(half, second_hop_compute)
-
-    third = third_hop(BATCH)
-    loop(half, third)
-
-    def third_hop_compute(i):
-        third(half + i)
-        compute(half + i)
-
-    loop(half, third_hop_compute)
-    loop(half, last_hop(BATCH, None))
-    loop(half, last_keep(BATCH))
-    finish(BATCH)(0)
-
-    done = finish(BATCH)
-
-    def done_compute(i):
-        done(i + 1)
-        compute(BATCH + 2 * i)
-        compute(BATCH + 2 * i + 1)
-
-    loop(half - 1, done_compute)
-    compute(CHUNKS - 2)
-    compute(CHUNKS - 1)
+    run(half, (fourth, 0))
+    run(half, (third, 1), (second, 2))
+    run(half, (finish, 0))
+    run(half, (lambda group, i: third(group, half + i), 1), (lambda group, i: second(group, half + i), 2))
+    run(half, (fourth, 1))
+    update(0, 0)
+    run(GROUP, (third, 2))
+    update(0, 1)
+    run(half, (fourth, 2))
+    run(half, (finish, 1))
+    update(1, 0)
+    run(half, (keep_third, 2))
+    update(1, 1)
+    run(half, (keep_fourth, 2))
+    loop(GROUP, lambda i: pair_arrived(2 * GROUP + i))
 
     sent = gathered.at[:, pl.ds(0, share * (depth - 1))]
     pltpu.make_async_copy(sent, sent, ring_send).wait()
@@ -252,19 +234,24 @@
     pltpu.make_async_copy(others, others, head_send).wait()
 
 
-def write_kernel(result, out, sem):
-    parts = 8
-    rows = result.shape[0] // parts
-    copies = [
-        pltpu.make_async_copy(
-            result.at[pl.ds(at * rows, rows)], out.at[pl.ds(at * rows, rows)], sem.at[at]
-        )
-        for at in range(parts)
-    ]
-    for copy in copies:
-        copy.start()
-    for copy in copies:
-        copy.wait()
+def last_kernel(result, gathered, upper_inv, mid, factors, out, last, sem):
+    rows = 2 * gathered.shape[2]
+    blocks = result.shape[0] // rows
+    ready = blocks - last.shape[0]
+
+    def copy(at):
+        source = result.at[pl.ds(at * rows, rows)] if at < ready else last.at[at - ready]
+        return pltpu.make_async_copy(source, out.at[pl.ds(at * rows, rows)], sem.at[at])
+
+    for at in range(ready):
+        copy(at).start()
+    for at in range(ready, blocks):
+        last[at - ready] = updated_rows(
+            gathered, 2 * at, result[pl.ds(at * rows, rows), :], upper_inv, mid, factors
+        )
+        copy(at).start()
+    for at in range(blocks):
+        copy(at).wait()
 
 
 def on_device(trailing_slab, panel_cols, head_slab, coupling, lower_inverses, upper_inverses):
@@ -273,19 +260,23 @@
     rows = height // CHUNKS
     dma = pltpu.SemaphoreType.DMA
     anywhere = pl.BlockSpec(memory_space=pltpu.HBM)
-    result = pl.pallas_call(
+    shape = jax.ShapeDtypeStruct
+    on_chip = pl.BlockSpec(memory_space=pltpu.VMEM)
+    kept = pl.pallas_call(
         update_kernel,
-        out_shape=jax.ShapeDtypeStruct((height, columns), BF16),
+        out_shape=[
+            shape((height, columns), BF16),
+            shape((CHUNKS, 2 * width, rows), BF16),
+            shape(upper_inverses.shape, BF16),
+            shape((width, width), BF16),
+            shape((2 * width, columns), BF16),
+        ],
         in_specs=[anywhere] * 6,
-        out_specs=pl.BlockSpec(memory_space=pltpu.VMEM),
+        out_specs=[on_chip] * 5,
         scratch_shapes=[
-            pltpu.VMEM((CHUNKS, 2 * width, rows), BF16),
             pltpu.VMEM((2 * width, columns), BF16),
             pltpu.VMEM(coupling.shape, BF16),
             pltpu.VMEM(lower_inverses.shape, BF16),
-            pltpu.VMEM(upper_inverses.shape, BF16),
-            pltpu.VMEM((width, width), BF16),
-            pltpu.VMEM((2 * width, columns), BF16),
             dma((6,)),
             dma(()),
             dma(()),
@@ -305,14 +296,17 @@
         )
     ])
     return pl.pallas_call(
-        write_kernel,
-        out_shape=jax.ShapeDtypeStruct((height, columns), BF16),
-        in_specs=[pl.BlockSpec(memory_space=pltpu.VMEM)],
+        last_kernel,
+        out_shape=shape((height, columns), BF16),
+        in_specs=[on_chip] * 5,
         out_specs=anywhere,
-        scratch_shapes=[dma((8,))],
-        compiler_params=pltpu.CompilerParams(vmem_limit_bytes=16 << 20),
-        name="write_result",
-    )(result)
+        scratch_shapes=[
+            pltpu.VMEM((GROUP // 2, 2 * rows, columns), BF16),
+            dma((CHUNKS // 2,)),
+        ],
+        compiler_params=pltpu.CompilerParams(vmem_limit_bytes=24 << 20),
+        name="update_last_and_write",
+    )(*kept)
 
 
 def solution(mesh):

time: 56.3 us -> 50.1 us (0.89)
  Pallas kernels: 56.2 us -> 50 us
    pallas_call x2, Pallas kernels: 56.2 us -> 50 us  [the longest x1 46.8 us: on_device(): pl.pallas_call(update_kernel, out_shape=[shape((height, columns), BF16),...]
where the time goes in v2:
time: 50.1 us; the launch traced here: 50 us
  Pallas kernels  50 us (100%)
    pallas_call x1, Pallas kernels, on_device(): pl.pallas_call(update_kernel, out_shape=[shape((height, columns), BF16),...  46.8 us
    pallas_call x1, Pallas kernels, on_device(): pl.pallas_call(last_kernel, out_shape=shape((height, columns), BF16), in_...  3.23 us

profile of v2, /device:TPU:1, one launch (start us, length us, event | category | flops | bytes accessed | tf_op | source)
XLA Modules:
  0.0 50.0 jit_solution(5139772562199782713)
XLA Ops:
  0.0 46.8 %gather_and_update.1 = (bf16[6144,512]{1,0:T(8,128)(2,1)S(1)}, bf16[12,512,512]{2,1,0:T(8,128)(2,1)S(1)}, bf16[2,256,256]{2,1,0:T(8,128)(2,1)S(1)}, bf16[256,256]{1,0:T(8,128)(2,1)S(1)}, bf16[512,512]{1,0:T(8,128)(2,1)S(1)}) custom-call(bf16[6144,512]{1,0:T(8,128)(2,1)} %slab_hbm.1, bf16[32,6144]{1,0:T(8,128)(2,1)} %bitcast.1, bf16[32,512]{1,0:T(8,128)(2,1)} %head_hbm.1, ...), custom_call_target="tpu_custom_call" | custom-call | tf_op jit(solution)/shard_map/gather_and_update/pallas_call | solution.py:265
  46.8 3.2 %update_last_and_write.1 = bf16[6144,512]{1,0:T(8,128)(2,1)} custom-call(bf16[6144,512]{1,0:T(8,128)(2,1)S(1)} %get-tuple-element.10.result, bf16[12,512,512]{2,1,0:T(8,128)(2,1)S(1)} %get-tuple-element.11.gathered, bf16[2,256,256]{2,1,0:T(8,128)(2,1)S(1)} %get-tuple-element.12.upper_inv, bf16[256,256]{1,0:T(8,128)(2,1)S(1)} %get-tuple-element.13.mid, ...), custom_call_target="tpu_custom_call" | custom-call | tf_op jit(solution)/shard_map/update_last_and_write/pallas_call | solution.py:298

commit v3 on v2

--- a/solution.py
+++ b/solution.py
@@ -33,7 +33,7 @@
     slab_hbm, panel_hbm, head_hbm, coupling_hbm, lower_hbm, upper_hbm,
     out, gathered, upper_inv, mid, factors,
     head_full, coupling, lower_inv,
-    local_sem, ring_send, pair_send, head_send, ring_recv, pair_recv, head_recv,
+    own_sem, local_sem, ring_send, pair_send, head_send, ring_recv, pair_recv, head_recv,
 ):
     chunks, width2, rows = gathered.shape
     width = width2 // 2
@@ -51,39 +51,37 @@
     barrier = pltpu.get_barrier_semaphore()
     for peer in (ahead, behind, other):
         pl.semaphore_signal(barrier, inc=1, device_id=(row, peer), device_id_type=MESH)
+
+    def block_rows(hops):
+        source = ((z + depth - hops) % depth) * 2 + core
+        return pl.ds(pl.multiple_of(source * share, share), share)
+
+    own_rows = block_rows(0)
+    head_rows = pl.ds(pl.multiple_of(row * head_share, head_share), head_share)
+
+    def own_copy(chunk):
+        return pltpu.make_async_copy(
+            panel_hbm.at[:, pl.ds(pl.multiple_of(chunk * rows, rows), rows)],
+            gathered.at[chunk, own_rows],
+            own_sem.at[chunk],
+        )
+
+    for chunk in range(chunks):
+        own_copy(chunk).start()
     for step in range(1, n_row):
         pl.semaphore_signal(
             barrier, inc=1, device_id=((row + step) % n_row, col), device_id_type=MESH
         )
 
-    def block_rows(hops):
-        source = ((z + depth - hops) % depth) * 2 + core
-        return pl.ds(pl.multiple_of(source * share, share), share)
-
-    own_rows = block_rows(0)
-    head_rows = pl.ds(pl.multiple_of(row * head_share, head_share), head_share)
-
-    for chunk in range(chunks):
-        pltpu.make_async_copy(
-            panel_hbm.at[:, pl.ds(chunk * rows, rows)],
-            gathered.at[chunk, own_rows],
-            local_sem.at[0],
-        ).start()
-    head_copy = pltpu.make_async_copy(head_hbm, head_full.at[head_rows], local_sem.at[1])
+    head_copy = pltpu.make_async_copy(head_hbm, head_full.at[head_rows], local_sem.at[0])
     head_copy.start()
     small_copies = [
         pltpu.make_async_copy(source, target, local_sem.at[at])
         for source, target, at in (
-            (coupling_hbm, coupling, 2), (lower_hbm, lower_inv, 3), (upper_hbm, upper_inv, 4),
-            (slab_hbm, out, 5),
+            (coupling_hbm, coupling, 1), (lower_hbm, lower_inv, 2), (upper_hbm, upper_inv, 3),
+            (slab_hbm, out, 4),
         )
     ]
-    for copy in small_copies:
-        copy.start()
-    pltpu.make_async_copy(
-        gathered.at[:, own_rows], gathered.at[:, own_rows], local_sem.at[0]
-    ).wait()
-    head_copy.wait()
     pl.semaphore_wait(barrier, 3 + n_row - 1)
 
     def ring_copy(direction, hop, chunk):
@@ -123,14 +121,18 @@
         )
 
     def send_own(chunk):
+        own_copy(chunk).wait()
         ring_copy(0, 1, chunk).start()
         ring_copy(1, 1, chunk).start()
         pair_copy(0, 0, chunk).start()
 
-    def forward(direction, hop, chunk):
-        ring_arrived(direction, hop, chunk)
-        ring_copy(direction, hop + 1, chunk).start()
-        pair_copy(direction, hop, chunk).start()
+    def forward(hop, chunk_up, chunk_down):
+        ring_arrived(0, hop, chunk_up)
+        ring_copy(0, hop + 1, chunk_up).start()
+        ring_arrived(1, hop, chunk_down)
+        ring_copy(1, hop + 1, chunk_down).start()
+        pair_copy(0, hop, chunk_up).start()
+        pair_copy(1, hop, chunk_down).start()
 
     def keep(direction, hop, chunk):
         ring_arrived(direction, hop, chunk)
@@ -151,18 +153,15 @@
         lax.fori_loop(0, count, lambda i, carry: (body(i), carry)[1], 0)
 
     def second(group, i):
-        forward(0, 1, group * GROUP + i)
-        forward(1, 1, group * GROUP + i)
+        forward(1, group * GROUP + i, group * GROUP + i)
 
     def third(group, i):
         base = group * GROUP
         turn = (2 * i) // GROUP
-        forward(0, 2, base + (2 * i) % GROUP + turn)
-        forward(1, 2, base + (2 * i + 1) % GROUP - turn)
+        forward(2, base + (2 * i) % GROUP + turn, base + (2 * i + 1) % GROUP - turn)
 
     def fourth(group, i):
-        forward(0, 3, group * GROUP + 2 * i)
-        forward(1, 3, group * GROUP + 2 * i + 1)
+        forward(3, group * GROUP + 2 * i, group * GROUP + 2 * i + 1)
 
     def keep_third(group, i):
         keep(1, 3, group * GROUP + 2 * i)
@@ -185,6 +184,9 @@
     half = GROUP // 2
 
     loop(2 * GROUP, send_own)
+    for copy in small_copies:
+        copy.start()
+    head_copy.wait()
     for step in range(1, n_row):
         pltpu.make_async_remote_copy(
             src_ref=head_full.at[head_rows],
@@ -215,16 +217,19 @@
     run(half, (third, 1), (second, 2))
     run(half, (finish, 0))
     run(half, (lambda group, i: third(group, half + i), 1), (lambda group, i: second(group, half + i), 2))
-    run(half, (fourth, 1))
+    run(half, (third, 2))
+    fourth(1, 0)
     update(0, 0)
-    run(GROUP, (third, 2))
+    third(2, 2)
+    fourth(1, 1)
+    third(2, 3)
     update(0, 1)
     run(half, (fourth, 2))
     run(half, (finish, 1))
+    run(half, (keep_third, 2))
     update(1, 0)
-    run(half, (keep_third, 2))
+    run(half, (keep_fourth, 2))
     update(1, 1)
-    run(half, (keep_fourth, 2))
     loop(GROUP, lambda i: pair_arrived(2 * GROUP + i))
 
     sent = gathered.at[:, pl.ds(0, share * (depth - 1))]
@@ -277,7 +282,8 @@
             pltpu.VMEM((2 * width, columns), BF16),
             pltpu.VMEM(coupling.shape, BF16),
             pltpu.VMEM(lower_inverses.shape, BF16),
-            dma((6,)),
+            dma((CHUNKS,)),
+            dma((5,)),
             dma(()),
             dma(()),
             dma(()),

time: 50.1 us -> 49.6 us (0.990)
    pallas_call x1, Pallas kernels: 46.8 us -> 46.2 us  [on_device(): pl.pallas_call(update_kernel, out_shape=[shape((height, columns), BF16),...]
where the time goes in v3:
time: 49.6 us; the launch traced here: 49.5 us
  Pallas kernels  49.5 us (100%)
    pallas_call x1, Pallas kernels, on_device(): pl.pallas_call(update_kernel, out_shape=[shape((height, columns), BF16),...  46.2 us
    pallas_call x1, Pallas kernels, on_device(): pl.pallas_call(last_kernel, out_shape=shape((height, columns), BF16), in_...  3.23 us

profile of v3, /device:TPU:1, one launch (start us, length us, event | category | flops | bytes accessed | tf_op | source)
XLA Modules:
  0.0 49.5 jit_solution(16153874395065449049)
XLA Ops:
  0.0 46.2 %gather_and_update.1 = (bf16[6144,512]{1,0:T(8,128)(2,1)S(1)}, bf16[12,512,512]{2,1,0:T(8,128)(2,1)S(1)}, bf16[2,256,256]{2,1,0:T(8,128)(2,1)S(1)}, bf16[256,256]{1,0:T(8,128)(2,1)S(1)}, bf16[512,512]{1,0:T(8,128)(2,1)S(1)}) custom-call(bf16[6144,512]{1,0:T(8,128)(2,1)} %slab_hbm.1, bf16[32,6144]{1,0:T(8,128)(2,1)} %bitcast.1, bf16[32,512]{1,0:T(8,128)(2,1)} %head_hbm.1, ...), custom_call_target="tpu_custom_call" | custom-call | tf_op jit(solution)/shard_map/gather_and_update/pallas_call | solution.py:270
  46.2 3.2 %update_last_and_write.1 = bf16[6144,512]{1,0:T(8,128)(2,1)} custom-call(bf16[6144,512]{1,0:T(8,128)(2,1)S(1)} %get-tuple-element.10.result, bf16[12,512,512]{2,1,0:T(8,128)(2,1)S(1)} %get-tuple-element.11.gathered, bf16[2,256,256]{2,1,0:T(8,128)(2,1)S(1)} %get-tuple-element.12.upper_inv, bf16[256,256]{1,0:T(8,128)(2,1)S(1)} %get-tuple-element.13.mid, ...), custom_call_target="tpu_custom_call" | custom-call | tf_op jit(solution)/shard_map/update_last_and_write/pallas_call | solution.py:304

commit v4 on v3

--- a/solution.py
+++ b/solution.py
@@ -79,9 +79,12 @@
         pltpu.make_async_copy(source, target, local_sem.at[at])
         for source, target, at in (
             (coupling_hbm, coupling, 1), (lower_hbm, lower_inv, 2), (upper_hbm, upper_inv, 3),
-            (slab_hbm, out, 4),
         )
     ]
+    def slab_copy(group, i):
+        where = pl.ds(pl.multiple_of((group * GROUP + i) * rows, rows), rows)
+        pltpu.make_async_copy(slab_hbm.at[where], out.at[where], local_sem.at[4]).start()
+
     pl.semaphore_wait(barrier, 3 + n_row - 1)
 
     def ring_copy(direction, hop, chunk):
@@ -201,8 +204,8 @@
     mid[...] = product(lower_inv[0], coupling[0]).astype(BF16)
     lower_head = product(coupling[1], upper_inv[0]).astype(BF16)
 
-    run(GROUP, (second, 0), (lambda group, i: send_own(group * GROUP + i), 2))
-    run(GROUP, (third, 0), (second, 1))
+    run(GROUP, (second, 0), (lambda group, i: send_own(group * GROUP + i), 2), (slab_copy, 0))
+    run(GROUP, (third, 0), (second, 1), (slab_copy, 1))
 
     others = head_full.at[pl.ds(0, head_share * (n_row - 1))]
     pltpu.make_async_copy(others, others, head_recv).wait()
@@ -214,11 +217,12 @@
     factors[width:] = product(lower_inv[1], head_second).astype(BF16)
 
     run(half, (fourth, 0))
-    run(half, (third, 1), (second, 2))
+    run(half, (third, 1), (second, 2), (slab_copy, 2), (lambda group, i: slab_copy(group, half + i), 2))
     run(half, (finish, 0))
     run(half, (lambda group, i: third(group, half + i), 1), (lambda group, i: second(group, half + i), 2))
     run(half, (third, 2))
     fourth(1, 0)
+    pltpu.make_async_copy(slab_hbm, out, local_sem.at[4]).wait()
     update(0, 0)
     third(2, 2)
     fourth(1, 1)

time: 49.6 us -> 49.6 us (level)
  no operation moved by 1% of the time
where the time goes in v4:
time: 49.6 us; the launch traced here: 49.5 us
  Pallas kernels  49.5 us (100%)
    pallas_call x1, Pallas kernels, on_device(): pl.pallas_call(update_kernel, out_shape=[shape((height, columns), BF16),...  46.2 us
    pallas_call x1, Pallas kernels, on_device(): pl.pallas_call(last_kernel, out_shape=shape((height, columns), BF16), in_...  3.23 us

profile of v4, /device:TPU:1, one launch (start us, length us, event | category | flops | bytes accessed | tf_op | source)
XLA Modules:
  0.0 49.5 jit_solution(1516247090926747788)
XLA Ops:
  0.0 46.2 %gather_and_update.1 = (bf16[6144,512]{1,0:T(8,128)(2,1)S(1)}, bf16[12,512,512]{2,1,0:T(8,128)(2,1)S(1)}, bf16[2,256,256]{2,1,0:T(8,128)(2,1)S(1)}, bf16[256,256]{1,0:T(8,128)(2,1)S(1)}, bf16[512,512]{1,0:T(8,128)(2,1)S(1)}) custom-call(bf16[6144,512]{1,0:T(8,128)(2,1)} %slab_hbm.1, bf16[32,6144]{1,0:T(8,128)(2,1)} %bitcast.1, bf16[32,512]{1,0:T(8,128)(2,1)} %head_hbm.1, ...), custom_call_target="tpu_custom_call" | custom-call | tf_op jit(solution)/shard_map/gather_and_update/pallas_call | solution.py:274
  46.2 3.2 %update_last_and_write.1 = bf16[6144,512]{1,0:T(8,128)(2,1)} custom-call(bf16[6144,512]{1,0:T(8,128)(2,1)S(1)} %get-tuple-element.10.result, bf16[12,512,512]{2,1,0:T(8,128)(2,1)S(1)} %get-tuple-element.11.gathered, bf16[2,256,256]{2,1,0:T(8,128)(2,1)S(1)} %get-tuple-element.12.upper_inv, bf16[256,256]{1,0:T(8,128)(2,1)S(1)} %get-tuple-element.13.mid, ...), custom_call_target="tpu_custom_call" | custom-call | tf_op jit(solution)/shard_map/update_last_and_write/pallas_call | solution.py:308

commit v5 on v3

--- a/solution.py
+++ b/solution.py
@@ -10,7 +10,7 @@
 MESH = pl.DeviceIdType.MESH
 BF16 = jnp.bfloat16
 F32 = jnp.float32
-GROUP = 4
+GROUP = 2
 GROUPS = 3
 CHUNKS = GROUP * GROUPS
 
@@ -21,7 +21,7 @@
 
 def updated_rows(gathered, chunk, slab_part, upper_inv, mid, factors):
     width = mid.shape[0]
-    panel = jnp.concatenate([gathered[chunk].T, gathered[chunk + 1].T], axis=0)
+    panel = gathered[chunk].T
     lower_first = product(panel[:, :width], upper_inv[0]).astype(BF16)
     second = (panel[:, width:].astype(F32) - product(lower_first, mid[...])).astype(BF16)
     lower_second = product(second, upper_inv[1]).astype(BF16)
@@ -143,10 +143,9 @@
         pltpu.make_async_copy(other_half, other_half, pair_recv.at[chunk]).wait()
 
     def update(group, i):
-        chunk = group * GROUP + 2 * i
+        chunk = group * GROUP + i
         pair_arrived(chunk)
-        pair_arrived(chunk + 1)
-        where = pl.ds(pl.multiple_of(chunk * rows, rows), 2 * rows)
+        where = pl.ds(pl.multiple_of(chunk * rows, rows), rows)
         out[where, :] = updated_rows(gathered, chunk, out[where, :], upper_inv, mid, factors)
 
     def loop(count, body):
@@ -220,9 +219,7 @@
     run(half, (third, 2))
     fourth(1, 0)
     update(0, 0)
-    third(2, 2)
-    fourth(1, 1)
-    third(2, 3)
+    third(2, 1)
     update(0, 1)
     run(half, (fourth, 2))
     run(half, (finish, 1))
@@ -240,7 +237,7 @@
 
 
 def last_kernel(result, gathered, upper_inv, mid, factors, out, last, sem):
-    rows = 2 * gathered.shape[2]
+    rows = gathered.shape[2]
     blocks = result.shape[0] // rows
     ready = blocks - last.shape[0]
 
@@ -252,7 +249,7 @@
         copy(at).start()
     for at in range(ready, blocks):
         last[at - ready] = updated_rows(
-            gathered, 2 * at, result[pl.ds(at * rows, rows), :], upper_inv, mid, factors
+            gathered, at, result[pl.ds(at * rows, rows), :], upper_inv, mid, factors
         )
         copy(at).start()
     for at in range(blocks):
@@ -307,8 +304,8 @@
         in_specs=[on_chip] * 5,
         out_specs=anywhere,
         scratch_shapes=[
-            pltpu.VMEM((GROUP // 2, 2 * rows, columns), BF16),
-            dma((CHUNKS // 2,)),
+            pltpu.VMEM((GROUP, rows, columns), BF16),
+            dma((CHUNKS,)),
         ],
         compiler_params=pltpu.CompilerParams(vmem_limit_bytes=24 << 20),
         name="update_last_and_write",

time: 49.6 us -> 50.7 us (1.022)
  Pallas kernels: 49.5 us -> 50.6 us
    pallas_call x1, Pallas kernels: 3.23 us -> 3.91 us  [on_device(): pl.pallas_call(last_kernel, out_shape=shape((height, columns), BF16), in_...]
where the time goes in v5:
time: 50.7 us; the launch traced here: 50.6 us
  Pallas kernels  50.6 us (100%)
    pallas_call x1, Pallas kernels, on_device(): pl.pallas_call(update_kernel, out_shape=[shape((height, columns), BF16),...  46.7 us
    pallas_call x1, Pallas kernels, on_device(): pl.pallas_call(last_kernel, out_shape=shape((height, columns), BF16), in_...  3.91 us

profile of v5, /device:TPU:1, one launch (start us, length us, event | category | flops | bytes accessed | tf_op | source)
XLA Modules:
  0.0 50.6 jit_solution(4275442592935047954)
XLA Ops:
  0.0 46.7 %gather_and_update.1 = (bf16[6144,512]{1,0:T(8,128)(2,1)S(1)}, bf16[6,512,1024]{2,1,0:T(8,128)(2,1)S(1)}, bf16[2,256,256]{2,1,0:T(8,128)(2,1)S(1)}, bf16[256,256]{1,0:T(8,128)(2,1)S(1)}, bf16[512,512]{1,0:T(8,128)(2,1)S(1)}) custom-call(bf16[6144,512]{1,0:T(8,128)(2,1)} %slab_hbm.1, bf16[32,6144]{1,0:T(8,128)(2,1)} %bitcast.1, bf16[32,512]{1,0:T(8,128)(2,1)} %head_hbm.1, ...), custom_call_target="tpu_custom_call" | custom-call | tf_op jit(solution)/shard_map/gather_and_update/pallas_call | solution.py:267
  46.7 3.9 %update_last_and_write.1 = bf16[6144,512]{1,0:T(8,128)(2,1)} custom-call(bf16[6144,512]{1,0:T(8,128)(2,1)S(1)} %get-tuple-element.10.result, bf16[6,512,1024]{2,1,0:T(8,128)(2,1)S(1)} %get-tuple-element.11.gathered, bf16[2,256,256]{2,1,0:T(8,128)(2,1)S(1)} %get-tuple-element.12.upper_inv, bf16[256,256]{1,0:T(8,128)(2,1)S(1)} %get-tuple-element.13.mid, ...), custom_call_target="tpu_custom_call" | custom-call | tf_op jit(solution)/shard_map/update_last_and_write/pallas_call | solution.py:301
